TPU v7x, 128 devices: a whole 4x4x4 slice. The times are simulated.
128 devices in a mesh: dp: 8 (over y, x_hi), fsdp: 16 (over z, x_lo, core).
Axes of the slice: x: 4 (x_hi: 2, x_lo: 2; x = x_hi * 2 + x_lo), y: 4, z: 4, core: 2. Of those that a mesh axis runs over, the one named last changes fastest.
Arguments:
- tokens: bfloat16 [49152, 8192], P(('dp', 'fsdp')), may hold values from -6 to 6
- frozen_value_weight: bfloat16 [8192, 1024], P('fsdp'), may hold values from -0.0625 to 0.0625
- adapter_down_weight: bfloat16 [32, 8192, 64], P('dp', 'fsdp'), may hold values from -0.0625 to 0.0625
- adapter_up_weight: bfloat16 [32, 64, 1024], P('dp', None, 'fsdp'), may hold values from -0.75 to 0.75
- output_gradient: bfloat16 [49152, 1024], P(('dp', 'fsdp')), may hold values from -6 to 6
- adapter_per_block: int32 [384], P(('dp', 'fsdp')), may hold values from 0 to 31, as said below
- block_live_count: int32 [384], P(('dp', 'fsdp')), may hold values from 1 to 128
Outputs:
- values: bfloat16 [49152, 1024], P(('dp', 'fsdp'))
- input_gradient: bfloat16 [49152, 8192], P(('dp', 'fsdp'))
- grad_down: float32 [32, 8192, 64], P('dp', 'fsdp')
- grad_up: float32 [32, 64, 1024], P('dp', None, 'fsdp')
Inputs may be any that keep to these rules, and one draw needn't show every extreme that they name: `adapter_per_block`: within the blocks of one device the adapter numbers never fall.
All inputs are finite; a program needn't handle non-finite values.
Results may differ from a plain program's by a relative error of at most 0.0038.
Values may be sent and summed in bfloat16 or wider, within the bound.
No kernel may reach another device: no remote copies, remote signals or barrier semaphores. Data moves between devices by JAX's collectives and lax.ppermute only.
A program may use at most 192 MiB of HBM per device.

v0:
```python
import jax
import jax.numpy as jnp
from jax import lax
from jax.sharding import PartitionSpec as P

adapter_scale = 0.5


def in_one_piece(arrays, axis, dim, along):
    ends, at = ([], 0)
    for a in arrays[:-1]:
        at += a.shape[along]
        ends.append(at)
    both = jnp.concatenate(arrays, axis=along)
    return tuple(jnp.split(lax.all_gather(both, axis, axis=dim, tiled=True), ends, axis=along))


def rows_first(arrays, axis, dims):
    turned = [jnp.moveaxis(a, dim, 0) for a, dim in zip(arrays, dims)]
    both = jnp.concatenate([t.reshape(len(t), -1) for t in turned], axis=1)
    result, at, outs = (lax.all_gather(both, axis, axis=0, tiled=True), 0, [])
    for t, dim in zip(turned, dims):
        piece = result[:, at : at + t[0].size].reshape(-1, *t.shape[1:])
        outs.append(jnp.moveaxis(piece, 0, dim))
        at += t[0].size
    return tuple(outs)


def cut_along(x, dim, devices):
    before, after = (x.shape[:dim], x.shape[dim + 1 :])
    return jnp.moveaxis(x.reshape(*before, devices, -1, *after), dim, 0)


def cut_rows(length, count):
    turn = length // count
    if turn >= 8:
        turn -= turn % 8
    return [turn * k for k in range(1, count)]


def in_order(parts, dim):
    parts = jnp.moveaxis(parts, 0, dim)
    dims = parts.shape
    return parts.reshape(*dims[:dim], dims[dim] * dims[dim + 1], *dims[dim + 2 :])


def several_exchanges(x, axis, pieces, split_dim, concat_dim):
    parts = cut_along(x, split_dim, lax.axis_size(axis))
    widest = max(range(1, max(2, parts.ndim - 1)), key=lambda d: parts.shape[d])
    outs = []
    for piece in jnp.split(parts, cut_rows(parts.shape[widest], pieces), axis=widest):
        if piece.size:
            outs.append(lax.all_to_all(piece, axis, split_axis=0, concat_axis=0, tiled=True))
    return in_order(jnp.concatenate(outs, axis=widest), concat_dim)


def in_one_piece_2(arrays, axis, dim, along):
    widths = [a.shape[along] for a in arrays]
    both = jnp.concatenate(arrays, axis=along)
    result = lax.psum_scatter(both, axis, scatter_dimension=dim, tiled=True)
    return tuple(jnp.split(result, [sum(widths[:k]) for k in range(1, len(widths))], axis=along))


def body(
    tokens,
    frozen_value_weight,
    adapter_down_weight,
    adapter_up_weight,
    output_gradient,
    adapter_per_block,
    block_live_count,
):
    count_dev = tokens.shape[0]
    per_dev = adapter_per_block.shape[0]
    block_rows = count_dev // per_dev
    adapter_list = adapter_down_weight.shape[0] * lax.axis_size("dp")
    piece = lax.all_gather(frozen_value_weight, "fsdp", axis=0, tiled=True)
    forward_pass = jnp.dot(tokens, piece, preferred_element_type=jnp.float32)
    portion_gradient = lax.dot_general(
        output_gradient, piece, (((1,), (1,)), ((), ())), preferred_element_type=jnp.float32
    )
    down_all, up_all = in_one_piece((adapter_down_weight, adapter_up_weight), "dp", 0, 1)
    ids_all, fill_all = rows_first((adapter_per_block, block_live_count), "fsdp", (0, 0))
    positions = jnp.arange(block_rows, dtype=jnp.int32)
    catalog = jnp.arange(adapter_list, dtype=jnp.int32)
    live_slot_mask = (positions[None, :] < fill_all[:, None]).astype(jnp.float32)[:, :, None]
    choose = (ids_all[:, None] == catalog[None, :]).astype(jnp.float32)
    down_per_block = down_all[ids_all]
    group_blocks = ids_all.shape[0]
    group_rows = group_blocks * block_rows
    x_group, dy_group = (
        lax.all_to_all(tokens, "fsdp", split_axis=1, concat_axis=0, tiled=True),
        lax.all_to_all(output_gradient, "fsdp", split_axis=1, concat_axis=0, tiled=True),
    )
    input_per_block = x_group.reshape(group_blocks, block_rows, -1)
    dy_blocks = dy_group.reshape(group_blocks, block_rows, -1)
    up_per_block = up_all[ids_all]
    down_partial = jnp.einsum(
        "gzq,gqx->gzx", input_per_block, down_per_block, preferred_element_type=jnp.float32
    )
    up_partial = jnp.einsum(
        "bkc,brc->bkr", dy_blocks, up_per_block, preferred_element_type=jnp.float32
    )
    down_total, up_total = lax.psum((down_partial, up_partial), "fsdp")
    reduced_down_output = (down_total * live_slot_mask).astype(jnp.bfloat16)
    reduced_output_gradient = (up_total * live_slot_mask).astype(jnp.bfloat16)
    raised_rows = (
        jnp.einsum(
            "bkr,brc->bkc", reduced_down_output, up_per_block, preferred_element_type=jnp.float32
        )
        .astype(jnp.bfloat16)
        .reshape(group_rows, -1)
    )
    spread_input = (
        jnp.einsum(
            "qjz,qaz->qja",
            reduced_output_gradient,
            down_per_block,
            preferred_element_type=jnp.float32,
        )
        .astype(jnp.bfloat16)
        .reshape(group_rows, -1)
    )
    raised_resident, input_resident = (
        several_exchanges(raised_rows, "fsdp", 2, 0, 1),
        several_exchanges(spread_input, "fsdp", 2, 0, 1),
    )
    up_terms = jnp.einsum(
        "bkr,bkc->brc", reduced_down_output, dy_blocks, preferred_element_type=jnp.float32
    )
    up_gradient = jnp.einsum("ba,brc->arc", choose, up_terms, precision=lax.Precision.HIGHEST)
    down_gradient_terms = jnp.einsum(
        "uia,uiw->uaw", input_per_block, reduced_output_gradient, preferred_element_type=jnp.float32
    )
    down_gradient = jnp.einsum(
        "ba,bdr->adr", choose, down_gradient_terms, precision=lax.Precision.HIGHEST
    )
    grad_down, grad_up = in_one_piece_2(
        (adapter_scale * down_gradient, adapter_scale * up_gradient), "dp", 0, 1
    )
    values = (forward_pass + adapter_scale * raised_resident.astype(jnp.float32)).astype(
        jnp.bfloat16
    )
    input_gradient = (portion_gradient + adapter_scale * input_resident.astype(jnp.float32)).astype(
        jnp.bfloat16
    )
    return (values, input_gradient, grad_down, grad_up)


def solution(mesh):
    placed = (
        P(("dp", "fsdp"), None),
        P("fsdp", None),
        P("dp", "fsdp", None),
        P("dp", None, "fsdp"),
        P(("dp", "fsdp"), None),
        P(("dp", "fsdp")),
        P(("dp", "fsdp")),
    )
    return jax.shard_map(
        body,
        mesh=mesh,
        in_specs=placed,
        out_specs=(
            P(("dp", "fsdp"), None),
            P(("dp", "fsdp"), None),
            P("dp", "fsdp", None),
            P("dp", None, "fsdp"),
        ),
        check_vma=False,
    )
```

profile of v0, /device:TPU:1, one launch (start us, length us, event | category | flops | bytes accessed | tf_op | source)
XLA Modules:
  0.0 559.3 jit_solution(6873364627100419224)
XLA Ops:
  7.2 2.3 copy.42
  9.5 7.8 %all-to-all-start.3 = ((bf16[384,16,64]{0,2,1:T(8,128)(2,1)}), bf16[384,16,64]{0,2,1:T(8,128)(2,1)S(1)}, u32[]{:S(2)}, u32[]{:S(2)}) async-start(bf16[384,16,64]{0,2,1:T(8,128)(2,1)} %bitcast.10), calls=%async_computation.3 | async-start | bytes 1572864 | tf_op jit(solution)/shard_map/all_to_all | solution.py:93
  17.2 6.2 %copy.68 = bf16[48,16,8,512]{3,2,0,1:T(8,128)(2,1)} copy(bf16[48,16,8,512]{3,2,1,0:T(8,128)(2,1)} %bitcast.57) | data formatting | bytes 12582912 | tf_op jit(solution)/shard_map/all_to_all | solution.py:92
  23.4 6.8 %all-to-all-done.3 = bf16[384,16,64]{0,2,1:T(8,128)(2,1)S(1)} async-done(((bf16[384,16,64]{0,2,1:T(8,128)(2,1)}), bf16[384,16,64]{0,2,1:T(8,128)(2,1)S(1)}, u32[]{:S(2)}, u32[]{:S(2)}) %all-to-all-start.3) | async-done | bytes 786464 | tf_op jit(solution)/shard_map/all_to_all | solution.py:93
  30.2 5.4 all-to-all-start
  35.8 0.8 pad_maximum_fusion.1
  36.6 99.6 %all-gather = s32[16,3,2]{1,2,0:T(2,128)S(1)} all-gather(s32[1,3,2]{1,2,0:T(2,128)S(1)} %add_bitcast_fusion), channel_id=1, replica_groups=mesh['dp'=8,'fsdp'=16] {'fsdp'}, dimensions={0}, use_global_device_ids=true | all-gather | bytes 408 | tf_op jit(solution)/shard_map/all_gather | solution.py:21
  136.8 1.3 reshape.63
  138.1 1.2 split.32
  139.3 1.6 gather_fusion.1
  140.9 1.6 split.33
  142.4 2.3 gather_fusion
  144.8 3.0 convolution_bitcast_fusion.1
  147.7 6.2 %convolution_bitcast_fusion.2 = f32[48,128,64]{1,2,0:T(8,128)} fusion(bf16[48,512,64]{1,2,0:T(8,128)(2,1)S(1)} %gather_fusion, bf16[48,128,512]{2,1,0:T(8,128)(2,1)} %bitcast.5), kind=kOutput, calls=%fused_computation.16 | convolution fusion | flops 402653184 | bytes 11010048 | tf_op jit(solution)/shard_map/gzq,gqx->gzx/dot_general | solution.py:98
  154.2 127.4 %all-reduce.3.cloned.1.call-done = (f32[48,128,64]{1,2,0:T(8,128)}, f32[48,128,64]{1,2,0:T(8,128)}) async-done(((f32[48,128,64]{1,2,0:T(8,128)}, f32[48,128,64]{1,2,0:T(8,128)}), (f32[48,128,64]{1,2,0:T(8,128)}, f32[48,128,64]{1,2,0:T(8,128)})) %all-reduce.3.cloned.1.call-update) | async-done | bytes 3145744 | tf_op jit(solution)/shard_map/psum | solution.py:104
  281.6 3.3 fusion.5
  284.9 3.2 copy.54
  288.1 4.4 convolution_bitcast_fusion
  292.5 0.7 convolution_multiply_fusion
  293.2 6.7 %fusion.2 = f32[32,512,64]{1,0,2:T(8,128)S(1)} fusion(f32[48,512,64]{1,2,0:T(8,128)S(1)} %convolution_bitcast_fusion, s32[48]{0:T(128)S(1)} %get-tuple-element.22), kind=kOutput, calls=%fused_computation.10 | convolution fusion | flops 605029888 | bytes 10485952 | tf_op jit(solution)/shard_map/ba,bdr->adr/dot_general | solution.py:135
  299.9 0.6 pad_maximum_fusion
  300.5 5.6 %copy.51 = f32[32,576,64]{1,2,0:T(8,128)} copy(f32[32,576,64]{1,0,2:T(8,128)S(1)} %pad_maximum_fusion) | data formatting | bytes 9437184 | tf_op jit(solution)/shard_map/concatenate | solution.py:59
  306.7 2.0 convolution_convert_fusion.1
  308.7 1.4 copy.38
  310.1 2.2 reshape_reshape.6
  312.3 2.3 fusion.16
  314.5 1.0 copy.39
  315.5 6.2 %all-to-all-start.1 = ((bf16[16,192,64]{1,2,0:T(8,128)(2,1)}), bf16[16,192,64]{1,2,0:T(8,128)(2,1)}, u32[]{:S(2)}, u32[]{:S(2)}) async-start(bf16[16,192,64]{1,2,0:T(8,128)(2,1)} %copy.39), calls=%async_computation.1 | async-start | bytes 1048576 | tf_op jit(solution)/shard_map/all_to_all | solution.py:53
  321.7 2.0 copy.40
  323.7 6.0 %convolution_convert_fusion = bf16[48,128,512]{2,1,0:T(8,128)(2,1)} fusion(bf16[48,512,64]{1,2,0:T(8,128)(2,1)S(1)} %gather_fusion, f32[48,128,64]{1,2,0:T(8,128)} %get-tuple-element.17, f32[48,128]{1,0:T(8,128)S(1)} %fusion.8), kind=kOutput, calls=%fused_computation.8 | convolution fusion | flops 406585344 | bytes 11034624 | tf_op jit(solution)/shard_map/qjz,qaz->qja/dot_general | solution.py:115
  329.7 3.9 all-to-all-done.1
  333.6 3.9 all-to-all-start.2
  337.5 6.3 %fusion.15 = (bf16[16,192,512]{2,1,0:T(8,128)(2,1)}, bf16[16,192,512]{2,1,0:T(8,128)(2,1)}) fusion(bf16[16,384,512]{2,1,0:T(8,128)(2,1)} %bitcast.55), kind=kLoop, calls=%fused_computation.35 | loop fusion | bytes 12582912 | tf_op jit(solution)/shard_map/split | solution.py:51
  343.8 7.0 %all-to-all-done.2 = bf16[16,192,64]{1,2,0:T(8,128)(2,1)S(1)} async-done(((bf16[16,192,64]{1,2,0:T(8,128)(2,1)}), bf16[16,192,64]{1,2,0:T(8,128)(2,1)S(1)}, u32[]{:S(2)}, u32[]{:S(2)}) %all-to-all-start.2) | async-done | bytes 393248 | tf_op jit(solution)/shard_map/all_to_all | solution.py:53
  350.8 0.8 copy-done.2
  351.6 49.6 %all_to_all.52 = bf16[16,192,512]{2,1,0:T(8,128)(2,1)S(1)} all-to-all(bf16[16,192,512]{2,1,0:T(8,128)(2,1)} %get-tuple-element.18), channel_id=1, replica_groups=mesh['dp'=8,'fsdp'=16] {'fsdp'}, dimensions={0} | all-to-all | bytes 6291456 | tf_op jit(solution)/shard_map/all_to_all | solution.py:53
  401.2 4.8 all-to-all-start.5
  406.0 2.7 convert_multiply_fusion
  408.7 3.1 copy.41
  411.7 42.0 %all-to-all-done.5 = bf16[16,192,512]{2,1,0:T(8,128)(2,1)} async-done(((bf16[16,192,512]{2,1,0:T(8,128)(2,1)}), bf16[16,192,512]{2,1,0:T(8,128)(2,1)}, u32[]{:S(2)}, u32[]{:S(2)}) %all-to-all-start.5) | async-done | bytes 3145760 | tf_op jit(solution)/shard_map/all_to_all | solution.py:53
  453.7 8.2 %multiply_bitcast_fusion = f32[16,48,8,512]{3,2,1,0:T(8,128)} fusion(bf16[16,192,512]{2,1,0:T(8,128)(2,1)} %all-to-all-done.5, bf16[16,192,512]{2,1,0:T(8,128)(2,1)S(1)} %all_to_all.52), kind=kLoop, calls=%fused_computation.3 | loop fusion | flops 15728640 | bytes 18874368
  461.9 11.8 %copy.58 = f32[16,48,8,512]{3,2,0,1:T(8,128)} copy(f32[16,48,8,512]{3,2,1,0:T(8,128)} %multiply_bitcast_fusion) | data formatting | bytes 25165824 | tf_op jit(solution)/shard_map/mul | solution.py:144
  473.6 0.9 split.39
  474.6 0.8 copy.52
  475.3 1.9 split.38
  477.2 48.3 %all-gather.4.cloned.1.call-done = bf16[8192,1024]{1,0:T(8,128)(2,1)} async-done(((bf16[512,1024]{1,0:T(8,128)(2,1)}), bf16[8192,1024]{1,0:T(8,128)(2,1)}) %all-gather.4.cloned.1.call-update) | async-done | bytes 16777232 | tf_op jit(solution)/shard_map/all_gather | solution.py:77
  525.5 12.8 %add_convert_fusion.1 = bf16[384,1024]{1,0:T(8,128)(2,1)} fusion(f32[384,1024]{1,0:T(8,128)S(1)} %copy-done.3, bf16[384,8192]{1,0:T(8,128)(2,1)} %param.7, bf16[8192,1024]{1,0:T(8,128)(2,1)} %all-gather.4.cloned.1.call-done), kind=kOutput, calls=%fused_computation.12 | convolution fusion | flops 6443237376 | bytes 25427968 | tf_op jit(solution)/shard_map/dot_general | solution.py:78
  538.3 14.5 %add_convert_fusion = bf16[384,8192]{1,0:T(8,128)(2,1)} fusion(f32[384,8192]{1,0:T(8,128)} %bitcast.56, bf16[384,1024]{1,0:T(8,128)(2,1)S(1)} %copy-done.4, bf16[8192,1024]{1,0:T(8,128)(2,1)} %all-gather.4.cloned.1.call-done), kind=kOutput, calls=%fused_computation.2 | convolution fusion | flops 6448742400 | bytes 36438016 | tf_op jit(solution)/shard_map/dot_general | solution.py:79
  (36 shorter events, 1.7 us)
Async XLA Ops:
  9.5 20.7 %all-to-all-start.3 = ((bf16[384,16,64]{0,2,1:T(8,128)(2,1)}), bf16[384,16,64]{0,2,1:T(8,128)(2,1)S(1)}, u32[]{:S(2)}, u32[]{:S(2)}) async-start(bf16[384,16,64]{0,2,1:T(8,128)(2,1)} %bitcast.10), calls=%async_computation.3 | async-start | bytes 1572864 | tf_op jit(solution)/shard_map/all_to_all | solution.py:93
  30.2 5.5 copy-start.6
  30.2 5.6 copy-start.5
  30.2 6.4 %copy-start.7 = (s32[3]{0:T(128)S(1)}, s32[3]{0:T(128)}, u32[]{:S(2)}) copy-start(s32[3]{0:T(128)} %param.13) | copy-start | bytes 40
  30.2 6.4 %copy-start.8 = (s32[3]{0:T(128)S(1)}, s32[3]{0:T(128)}, u32[]{:S(2)}) copy-start(s32[3]{0:T(128)} %param.12) | copy-start | bytes 40
  30.2 117.5 %all-to-all-start = ((bf16[384,16,512]{2,0,1:T(8,128)(2,1)}), bf16[384,16,512]{2,0,1:T(8,128)(2,1)}, u32[]{:S(2)}, u32[]{:S(2)}) async-start(bf16[384,16,512]{2,0,1:T(8,128)(2,1)} %bitcast.54), calls=%async_computation | async-start | bytes 12582912 | tf_op jit(solution)/shard_map/all_to_all | solution.py:92
  35.6 102.5 %all-gather.6.cloned.1.call-start = ((), (), s32[]{:S(2)}) async-start(), calls=%async_computation.8 | async-start | bytes 2949120 | tf_op jit(solution)/shard_map/all_gather | solution.py:15
  36.6 245.1 %all-reduce.3.cloned.1.call-start = ((), (), s32[]{:S(2)}) async-start(), calls=%async_computation.10 | async-start | bytes 6291456 | tf_op jit(solution)/shard_map/psum | solution.py:104
  138.1 2.8 copy-start.1
  153.9 319.7 %reduce-scatter.2.cloned.1.call-start = ((), (), s32[]{:S(2)}) async-start(), calls=%async_computation.9 | async-start | bytes 5898240 | tf_op jit(solution)/shard_map/reduce_scatter | solution.py:60
  288.1 4.4 copy-start
  306.1 219.3 %all-gather.4.cloned.1.call-start = ((), (), s32[]{:S(2)}) async-start(), calls=%async_computation.7 | async-start | bytes 17825792 | tf_op jit(solution)/shard_map/all_gather | solution.py:77
  315.5 18.1 %all-to-all-start.1 = ((bf16[16,192,64]{1,2,0:T(8,128)(2,1)}), bf16[16,192,64]{1,2,0:T(8,128)(2,1)}, u32[]{:S(2)}, u32[]{:S(2)}) async-start(bf16[16,192,64]{1,2,0:T(8,128)(2,1)} %copy.39), calls=%async_computation.1 | async-start | bytes 1048576 | tf_op jit(solution)/shard_map/all_to_all | solution.py:53
  333.6 17.2 %all-to-all-start.2 = ((bf16[16,192,64]{1,2,0:T(8,128)(2,1)}), bf16[16,192,64]{1,2,0:T(8,128)(2,1)S(1)}, u32[]{:S(2)}, u32[]{:S(2)}) async-start(bf16[16,192,64]{1,2,0:T(8,128)(2,1)} %copy.40), calls=%async_computation.2 | async-start | bytes 1048576 | tf_op jit(solution)/shard_map/all_to_all | solution.py:53
  350.8 0.8 copy-start.2
  401.2 52.5 %all-to-all-start.5 = ((bf16[16,192,512]{2,1,0:T(8,128)(2,1)}), bf16[16,192,512]{2,1,0:T(8,128)(2,1)}, u32[]{:S(2)}, u32[]{:S(2)}) async-start(bf16[16,192,512]{2,1,0:T(8,128)(2,1)} %get-tuple-element.19), calls=%async_computation.5 | async-start | bytes 6291456 | tf_op jit(solution)/shard_map/all_to_all | solution.py:53
  461.9 63.6 %copy-start.3 = (f32[384,1024]{1,0:T(8,128)S(1)}, f32[384,1024]{1,0:T(8,128)}, u32[]{:S(2)}) copy-start(f32[384,1024]{1,0:T(8,128)} %copy.41) | copy-start | bytes 4718596
  477.2 61.1 %copy-start.4 = (bf16[384,1024]{1,0:T(8,128)(2,1)S(1)}, bf16[384,1024]{1,0:T(8,128)(2,1)}, u32[]{:S(2)}) copy-start(bf16[384,1024]{1,0:T(8,128)(2,1)} %param.11) | copy-start | bytes 2359300
Sparse Core Ops, SparseCore 0:
  39.3 76.9 all-gather.5
  154.1 127.5 all-reduce.2
  306.2 116.6 reduce-scatter.1
  424.5 100.9 all-gather.3
where the time goes:
time: 560 us; the launch traced here: 559 us
  waiting for transfers between devices  236 us (42%)
  blocking collectives  149 us (27%)
  local copies, waits for them, and re-layouts  60.1 us (11%)
  matrix products  59.4 us (11%)
  starting transfers between devices  28.5 us (5%)
  between operations  13.9 us (2%)
  other arithmetic  12.3 us (2%)
    psum x1, waiting for transfers between devices, body(): down_total, up_total = lax.psum((down_partial, up_partial), 'fsdp')  127 us
    all_gather x1, blocking collectives, rows_first(): result, at, outs = (lax.all_gather(both, axis, axis=0, tiled=True), 0, [])  99.6 us
    all_to_all x3, waiting for transfers between devices, several_exchanges(): lax.all_to_all(piece, axis, split_axis=0, concat_axis=0, tiled=True)  52.9 us
    all_to_all x1, blocking collectives, several_exchanges(): lax.all_to_all(piece, axis, split_axis=0, concat_axis=0, tiled=True)  49.6 us
    all_gather x1, waiting for transfers between devices, body(): piece = lax.all_gather(frozen_value_weight, 'fsdp', axis=0, tiled=True)  48.3 us
    all_to_all x3, starting transfers between devices, several_exchanges(): lax.all_to_all(piece, axis, split_axis=0, concat_axis=0, tiled=True)  15 us
    dot_general x1, matrix products, body(): lax.dot_general(output_gradient, piece, (((1,), (1,)), ((), ())), preferr...  14.5 us
    dot_general x1, matrix products, body(): forward_pass = jnp.dot(tokens, piece, preferred_element_type=jnp.float32)  12.8 us
  transfers between devices with their start and end apart: 9, of which 6 were waited for; matrix products, arithmetic and copies ran while one was open for 13% of the time, Pallas kernels for 0%

commit v1 on v0

--- a/solution.py
+++ b/solution.py
@@ -74,7 +74,8 @@
     per_dev = adapter_per_block.shape[0]
     block_rows = count_dev // per_dev
     adapter_list = adapter_down_weight.shape[0] * lax.axis_size("dp")
-    piece = lax.all_gather(frozen_value_weight, "fsdp", axis=0, tiled=True)
+    sent = jnp.stack([frozen_value_weight] * lax.axis_size("fsdp"))
+    piece = jnp.concatenate(lax.all_to_all(sent, "fsdp", 0, 0), axis=0)
     forward_pass = jnp.dot(tokens, piece, preferred_element_type=jnp.float32)
     portion_gradient = lax.dot_general(
         output_gradient, piece, (((1,), (1,)), ((), ())), preferred_element_type=jnp.float32

time: 560 us -> 677 us (1.21)
  waiting for transfers between devices: 236 us -> 309 us
  blocking collectives: 149 us -> 185 us
    all_to_all x0 -> x1, waiting for transfers between devices: none -> 169 us  [body(): piece = jnp.concatenate(lax.all_to_all(sent, 'fsdp', 0, 0), axis=0)]
    all_gather x1 -> x0, waiting for transfers between devices: 48.3 us -> none  [body(): piece = lax.all_gather(frozen_value_weight, 'fsdp', axis=0, tiled=True)]
    all_to_all x3 -> x2, waiting for transfers between devices: 52.9 us -> 5.78 us  [several_exchanges(): lax.all_to_all(piece, axis, split_axis=0, concat_axis=0, tiled=True)]
    all_to_all x1 -> x2, blocking collectives: 49.6 us -> 85.3 us  [several_exchanges(): lax.all_to_all(piece, axis, split_axis=0, concat_axis=0, tiled=True)]
    all_to_all x3 -> x2, starting transfers between devices: 15 us -> 10.8 us  [several_exchanges(): lax.all_to_all(piece, axis, split_axis=0, concat_axis=0, tiled=True)]
  transfers between devices with their start and end apart: 9 -> 8, of which waited for: 6 -> 5; matrix products, arithmetic and copies ran while one was open for 13% -> 16% of each run, Pallas kernels for 0% -> 0%
where the time goes in v1:
time: 677 us; the launch traced here: 676 us
  waiting for transfers between devices  309 us (46%)
  blocking collectives  185 us (27%)
  local copies, waits for them, and re-layouts  65.5 us (10%)
  matrix products  60.4 us (9%)
  starting transfers between devices  30.2 us (4%)
  between operations  13.9 us (2%)
  other arithmetic  12.3 us (2%)
    all_to_all x1, waiting for transfers between devices, body(): piece = jnp.concatenate(lax.all_to_all(sent, 'fsdp', 0, 0), axis=0)  169 us
    psum x1, waiting for transfers between devices, body(): down_total, up_total = lax.psum((down_partial, up_partial), 'fsdp')  127 us
    all_gather x1, blocking collectives, rows_first(): result, at, outs = (lax.all_gather(both, axis, axis=0, tiled=True), 0, [])  99.6 us
    all_to_all x2, blocking collectives, several_exchanges(): lax.all_to_all(piece, axis, split_axis=0, concat_axis=0, tiled=True)  85.3 us
    dot_general x1, matrix products, body(): lax.dot_general(output_gradient, piece, (((1,), (1,)), ((), ())), preferr...  14.6 us
  transfers between devices with their start and end apart: 8, of which 5 were waited for; matrix products, arithmetic and copies ran while one was open for 16% of the time, Pallas kernels for 0%

profile of v1, /device:TPU:1, one launch (start us, length us, event | category | flops | bytes accessed | tf_op | source)
XLA Modules:
  0.0 675.9 jit_solution(9823186002811572232)
XLA Ops:
  7.2 2.3 copy.42
  9.5 7.8 %all-to-all-start.4 = ((bf16[384,16,64]{0,2,1:T(8,128)(2,1)}), bf16[384,16,64]{0,2,1:T(8,128)(2,1)S(1)}, u32[]{:S(2)}, u32[]{:S(2)}) async-start(bf16[384,16,64]{0,2,1:T(8,128)(2,1)} %bitcast.11), calls=%async_computation.4 | async-start | bytes 1572864 | tf_op jit(solution)/shard_map/all_to_all | solution.py:94
  17.2 6.2 copy.68
  23.4 6.8 %all-to-all-done.4 = bf16[384,16,64]{0,2,1:T(8,128)(2,1)S(1)} async-done(((bf16[384,16,64]{0,2,1:T(8,128)(2,1)}), bf16[384,16,64]{0,2,1:T(8,128)(2,1)S(1)}, u32[]{:S(2)}, u32[]{:S(2)}) %all-to-all-start.4) | async-done | bytes 786464 | tf_op jit(solution)/shard_map/all_to_all | solution.py:94
  30.2 5.4 all-to-all-start.1
  35.8 0.8 pad_maximum_fusion.1
  36.6 99.6 %all-gather = s32[16,3,2]{1,2,0:T(2,128)S(1)} all-gather(s32[1,3,2]{1,2,0:T(2,128)S(1)} %add_bitcast_fusion), channel_id=1, replica_groups=mesh['dp'=8,'fsdp'=16] {'fsdp'}, dimensions={0}, use_global_device_ids=true | all-gather | bytes 408 | tf_op jit(solution)/shard_map/all_gather | solution.py:21
  136.8 1.3 reshape.69
  138.1 1.2 split.32
  139.3 1.6 gather_fusion.1
  140.9 1.5 split.33
  142.4 2.3 gather_fusion
  144.8 3.0 convolution_bitcast_fusion.1
  147.7 6.2 convolution_bitcast_fusion.2
  154.0 127.1 %all-reduce.3.cloned.1.call-done = (f32[48,128,64]{1,2,0:T(8,128)}, f32[48,128,64]{1,2,0:T(8,128)}) async-done(((f32[48,128,64]{1,2,0:T(8,128)}, f32[48,128,64]{1,2,0:T(8,128)}), (f32[48,128,64]{1,2,0:T(8,128)}, f32[48,128,64]{1,2,0:T(8,128)})) %all-reduce.3.cloned.1.call-update) | async-done | bytes 3145744 | tf_op jit(solution)/shard_map/psum | solution.py:105
  281.1 2.0 convolution_convert_fusion.1
  283.1 1.4 copy.38
  284.5 2.2 reshape_reshape.6
  286.7 2.3 fusion.16
  288.9 1.0 copy.39
  289.9 6.2 all-to-all-start.2
  296.1 2.0 copy.40
  298.1 5.9 convolution_convert_fusion
  304.1 2.0 all-to-all-done.2
  306.1 4.5 all-to-all-start.3
  310.6 6.1 fusion.15
  316.8 3.7 all-to-all-done.3
  320.5 0.8 copy-done.3
  321.3 42.9 %all_to_all.57 = bf16[16,192,512]{2,1,0:T(8,128)(2,1)S(1)} all-to-all(bf16[16,192,512]{2,1,0:T(8,128)(2,1)} %get-tuple-element.18), channel_id=1, replica_groups=mesh['dp'=8,'fsdp'=16] {'fsdp'}, dimensions={0} | all-to-all | bytes 6291456 | tf_op jit(solution)/shard_map/all_to_all | solution.py:53
  364.2 42.4 %all_to_all.58 = bf16[16,192,512]{2,1,0:T(8,128)(2,1)} all-to-all(bf16[16,192,512]{2,1,0:T(8,128)(2,1)S(1)} %copy-done), channel_id=1, replica_groups=mesh['dp'=8,'fsdp'=16] {'fsdp'}, dimensions={0} | all-to-all | bytes 6291456 | tf_op jit(solution)/shard_map/all_to_all | solution.py:53
  406.7 6.0 stack.2
  412.6 6.0 all-to-all-start
  418.9 3.3 fusion.5
  422.2 3.2 copy.54
  425.4 2.2 convolution_multiply_fusion
  427.6 3.8 convolution_bitcast_fusion
  431.4 6.7 fusion.2
  438.7 5.7 copy.51
  444.3 2.7 convert_multiply_fusion
  447.0 3.0 copy.41
  450.0 8.2 %multiply_bitcast_fusion = f32[16,48,8,512]{3,2,1,0:T(8,128)} fusion(bf16[16,192,512]{2,1,0:T(8,128)(2,1)} %all_to_all.58, bf16[16,192,512]{2,1,0:T(8,128)(2,1)S(1)} %all_to_all.57), kind=kLoop, calls=%fused_computation.3 | loop fusion | flops 15728640 | bytes 18874368
  458.2 11.4 %copy.58 = f32[16,48,8,512]{3,2,0,1:T(8,128)} copy(f32[16,48,8,512]{3,2,1,0:T(8,128)} %multiply_bitcast_fusion) | data formatting | bytes 25165824 | tf_op jit(solution)/shard_map/mul | solution.py:145
  469.7 168.8 %all-to-all-done = bf16[16,512,1024]{2,1,0:T(8,128)(2,1)} async-done(((bf16[16,512,1024]{2,1,0:T(8,128)(2,1)}), bf16[16,512,1024]{2,1,0:T(8,128)(2,1)}, u32[]{:S(2)}, u32[]{:S(2)}) %all-to-all-start) | async-done | bytes 16777248 | tf_op jit(solution)/shard_map/all_to_all | solution.py:78
  638.4 14.6 %add_convert_fusion = bf16[384,8192]{1,0:T(8,128)(2,1)} fusion(f32[384,8192]{1,0:T(8,128)} %bitcast.57, bf16[384,1024]{1,0:T(8,128)(2,1)S(1)} %copy-done.6, bf16[8192,1024]{1,0:T(8,128)(2,1)} %bitcast), kind=kOutput, calls=%fused_computation.2 | convolution fusion | flops 6448742400 | bytes 36438016 | tf_op jit(solution)/shard_map/dot_general | solution.py:80
  653.0 12.8 %add_convert_fusion.1 = bf16[384,1024]{1,0:T(8,128)(2,1)} fusion(f32[384,1024]{1,0:T(8,128)S(1)} %copy-done.4, bf16[384,8192]{1,0:T(8,128)(2,1)} %param.7, bf16[8192,1024]{1,0:T(8,128)(2,1)} %bitcast), kind=kOutput, calls=%fused_computation.12 | convolution fusion | flops 6443237376 | bytes 25427968 | tf_op jit(solution)/shard_map/dot_general | solution.py:79
  665.8 0.9 split.39
  666.7 0.8 copy.52
  667.5 1.9 split.38
  (39 shorter events, 1.7 us)
Async XLA Ops:
  9.5 20.7 %all-to-all-start.4 = ((bf16[384,16,64]{0,2,1:T(8,128)(2,1)}), bf16[384,16,64]{0,2,1:T(8,128)(2,1)S(1)}, u32[]{:S(2)}, u32[]{:S(2)}) async-start(bf16[384,16,64]{0,2,1:T(8,128)(2,1)} %bitcast.11), calls=%async_computation.4 | async-start | bytes 1572864 | tf_op jit(solution)/shard_map/all_to_all | solution.py:94
  30.2 5.4 copy-start.8
  30.2 5.6 copy-start.7
  30.2 6.4 copy-start.9
  30.2 6.4 copy-start.10
  30.2 117.5 %all-to-all-start.1 = ((bf16[384,16,512]{2,0,1:T(8,128)(2,1)}), bf16[384,16,512]{2,0,1:T(8,128)(2,1)}, u32[]{:S(2)}, u32[]{:S(2)}) async-start(bf16[384,16,512]{2,0,1:T(8,128)(2,1)} %bitcast.55), calls=%async_computation.1 | async-start | bytes 12582912 | tf_op jit(solution)/shard_map/all_to_all | solution.py:93
  35.6 102.5 %all-gather.3.cloned.1.call-start = ((), (), s32[]{:S(2)}) async-start(), calls=%async_computation.8 | async-start | bytes 2949120 | tf_op jit(solution)/shard_map/all_gather | solution.py:15
  36.5 244.6 %all-reduce.3.cloned.1.call-start = ((), (), s32[]{:S(2)}) async-start(), calls=%async_computation.10 | async-start | bytes 6291456 | tf_op jit(solution)/shard_map/psum | solution.py:105
  138.1 2.8 copy-start.2
  289.9 16.2 %all-to-all-start.2 = ((bf16[16,192,64]{1,2,0:T(8,128)(2,1)}), bf16[16,192,64]{1,2,0:T(8,128)(2,1)}, u32[]{:S(2)}, u32[]{:S(2)}) async-start(bf16[16,192,64]{1,2,0:T(8,128)(2,1)} %copy.39), calls=%async_computation.2 | async-start | bytes 1048576 | tf_op jit(solution)/shard_map/all_to_all | solution.py:53
  306.1 14.4 %all-to-all-start.3 = ((bf16[16,192,64]{1,2,0:T(8,128)(2,1)}), bf16[16,192,64]{1,2,0:T(8,128)(2,1)S(1)}, u32[]{:S(2)}, u32[]{:S(2)}) async-start(bf16[16,192,64]{1,2,0:T(8,128)(2,1)} %copy.40), calls=%async_computation.3 | async-start | bytes 1048576 | tf_op jit(solution)/shard_map/all_to_all | solution.py:53
  320.5 0.8 copy-start.3
  321.3 42.9 %copy-start = (bf16[16,192,512]{2,1,0:T(8,128)(2,1)S(1)}, bf16[16,192,512]{2,1,0:T(8,128)(2,1)}, u32[]{:S(2)}) copy-start(bf16[16,192,512]{2,1,0:T(8,128)(2,1)} %get-tuple-element.19) | copy-start | bytes 9437188
  364.2 42.4 %copy-start.5 = (bf16[512,1024]{1,0:T(8,128)(2,1)S(1)}, bf16[512,1024]{1,0:T(8,128)(2,1)}, u32[]{:S(2)}) copy-start(bf16[512,1024]{1,0:T(8,128)(2,1)} %param.8) | copy-start | bytes 3145732
  412.6 225.8 %all-to-all-start = ((bf16[16,512,1024]{2,1,0:T(8,128)(2,1)}), bf16[16,512,1024]{2,1,0:T(8,128)(2,1)}, u32[]{:S(2)}, u32[]{:S(2)}) async-start(bf16[16,512,1024]{2,1,0:T(8,128)(2,1)} %stack.2), calls=%async_computation | async-start | bytes 33554432 | tf_op jit(solution)/shard_map/all_to_all | solution.py:78
  418.7 247.1 %reduce-scatter.2.cloned.1.call-start = ((), (), s32[]{:S(2)}) async-start(), calls=%async_computation.9 | async-start | bytes 5898240 | tf_op jit(solution)/shard_map/reduce_scatter | solution.py:60
  425.4 2.2 copy-start.1
  458.2 180.2 %copy-start.6 = (bf16[384,1024]{1,0:T(8,128)(2,1)S(1)}, bf16[384,1024]{1,0:T(8,128)(2,1)}, u32[]{:S(2)}) copy-start(bf16[384,1024]{1,0:T(8,128)(2,1)} %param.11) | copy-start | bytes 2359300
  638.4 14.6 %copy-start.4 = (f32[384,1024]{1,0:T(8,128)S(1)}, f32[384,1024]{1,0:T(8,128)}, u32[]{:S(2)}) copy-start(f32[384,1024]{1,0:T(8,128)} %copy.41) | copy-start | bytes 4718596
Sparse Core Ops, SparseCore 0:
  39.3 76.9 all-gather.2
  154.1 126.9 all-reduce.2
  444.4 131.9 reduce-scatter.1
